TPU v7x, 128 devices: a whole 4x4x4 slice. The times are simulated.
128 devices in a mesh: segment: 8 (over x, core), patch: 16 (over y, z).
Axes of the slice: x: 4, y: 4, z: 4, core: 2. Of those that a mesh axis runs over, the one named last changes fastest.
Arguments:
- latent: bfloat16 [2, 64, 64, 640], P(None, 'patch'), may hold values from -6 to 6
- stale_attn: bfloat16 [8, 2, 64, 64, 640], P('segment', None, 'patch'), may hold values from -6 to 6
- stale_edge: bfloat16 [8, 2, 32, 64, 640], P('segment', None, 'patch'), may hold values from -6 to 6
- norm_attn: float32 [8, 640], P('segment'), may hold values from 0.1 to 1.9
- query_w: bfloat16 [8, 640, 640], P('segment'), may hold values from -0.5 to 0.5
- key_w: bfloat16 [8, 640, 640], P('segment'), may hold values from -0.25 to 0.25
- value_w: bfloat16 [8, 640, 640], P('segment'), may hold values from -0.25 to 0.25
- out_w: bfloat16 [8, 640, 640], P('segment'), may hold values from -0.75 to 0.75
- norm_conv: float32 [8, 640], P('segment'), may hold values from 0.1 to 1.9
- conv_w: bfloat16 [8, 3, 3, 640, 640], P('segment'), may hold values from -0.078125 to 0.078125
Outputs:
- denoised: float32 [2, 64, 64, 640], P(None, 'patch', 'segment')
All inputs are finite; a program needn't handle non-finite values.
Results may differ from a plain program's by a relative error of at most 0.035.
Values may be sent and summed in bfloat16 or wider, within the bound.
No kernel may reach another device: no remote copies, remote signals or barrier semaphores. Data moves between devices by JAX's collectives and lax.ppermute only.
A program may use at most 128 MiB of HBM per device.

v0:
```python
import jax
import jax.numpy as jnp
from jax import lax
from jax.sharding import PartitionSpec as P

HEADS = 10


def padded(cells, sides, width):
    for axis, dim in sides:
        count = lax.axis_size(axis)
        ends = count - 1
        head = lax.slice_in_dim(cells, 0, width, axis=dim)
        tail = lax.slice_in_dim(cells, cells.shape[dim] - width, cells.shape[dim], axis=dim)
        cells = jnp.concatenate(
            [
                lax.ppermute(tail, axis, [(i, (i + 1) % count) for i in range(ends)]),
                cells,
                lax.ppermute(head, axis, [((i + 1) % count, i) for i in range(ends)]),
            ],
            axis=dim,
        )
    return cells


def passed_along(value, axis, by):
    length = lax.axis_size(axis)
    pairs = [(i, i + by) for i in range(length) if 0 <= i + by < length]
    return lax.ppermute(value, axis, pairs)


def layer_norm(values, gain_vec):
    floats = values.astype(jnp.float32)
    center = floats - jnp.mean(floats, axis=-1, keepdims=True)
    spread = jnp.mean(center * center, axis=-1, keepdims=True)
    return center * lax.rsqrt(spread + 1e-05) * gain_vec


def project(row_data, weight):
    flattened = row_data.reshape(-1, row_data.shape[-1])
    result = jnp.dot(flattened, weight, preferred_element_type=jnp.float32).astype(jnp.bfloat16)
    return result.reshape(row_data.shape[:-1] + (weight.shape[1],))


def shards(
    latent, stale_attn, stale_edge, norm_attn, query_w, key_w, value_w, out_w, norm_conv, conv_w
):
    segment_index = lax.axis_index("segment")
    segment_count = lax.axis_size("segment")
    patch_index = lax.axis_index("patch")
    micro_count, row_count, col_count, channels = latent.shape
    head_count = HEADS
    head_dim = channels // head_count
    cell_count = row_count * col_count
    score_scale = head_dim ** (-0.5)
    gain_attn = norm_attn[0]
    gain_conv = norm_conv[0]
    query_weight = query_w[0]
    key_weight = key_w[0]
    value_weight = value_w[0]
    out_weight = out_w[0]
    kernel = conv_w[0]
    stale_normed = layer_norm(stale_attn[0], gain_attn).astype(jnp.bfloat16)
    near_keys = project(stale_normed, key_weight)
    near_values = project(stale_normed, value_weight)
    far_keys, far_values = (
        lax.all_gather(near_keys, "patch", axis=1, tiled=True),
        lax.all_gather(near_values, "patch", axis=1, tiled=True),
    )
    far_keys = far_keys.reshape(micro_count, -1, channels)
    far_values = far_values.reshape(micro_count, -1, channels)
    key_block = 4 * cell_count
    block_total = far_keys.shape[1] // key_block
    edge_rows = padded(stale_edge[0], (("patch", 1),), 1)

    def attend(queries, fresh_key, fresh_value, micro_pos):
        query_heads = queries.reshape(cell_count, head_count, head_dim)
        keys_now = lax.dynamic_index_in_dim(far_keys, micro_pos, 0, keepdims=False)
        values_now = lax.dynamic_index_in_dim(far_values, micro_pos, 0, keepdims=False)
        own_keys = fresh_key.reshape(cell_count, head_count, head_dim)
        own_values = fresh_value.reshape(cell_count, head_count, head_dim)
        own_scores = (
            jnp.einsum("qhd,khd->hqk", query_heads, own_keys, preferred_element_type=jnp.float32)
            * score_scale
        )
        own_exp = jnp.exp(own_scores)
        totals = jnp.sum(own_exp, axis=-1)
        context_sum = jnp.einsum(
            "hqk,khd->qhd",
            own_exp.astype(jnp.bfloat16),
            own_values,
            preferred_element_type=jnp.float32,
        )

        def add_block(block_no, carry):
            sums, partial_value = carry
            key_part = lax.dynamic_slice_in_dim(
                keys_now, block_no * key_block, key_block, 0
            ).reshape(key_block, head_count, head_dim)
            value_part = lax.dynamic_slice_in_dim(
                values_now, block_no * key_block, key_block, 0
            ).reshape(key_block, head_count, head_dim)
            scores = (
                jnp.einsum(
                    "qhd,khd->hqk", query_heads, key_part, preferred_element_type=jnp.float32
                )
                * score_scale
            )
            owner_patch = (
                block_no * key_block + jnp.arange(key_block, dtype=jnp.int32)
            ) // cell_count
            kept_mask = (owner_patch != patch_index).astype(jnp.float32)
            exp_scores = jnp.exp(scores) * kept_mask
            sums = sums + jnp.sum(exp_scores, axis=-1)
            partial_value = partial_value + jnp.einsum(
                "hqk,khd->qhd",
                exp_scores.astype(jnp.bfloat16),
                value_part,
                preferred_element_type=jnp.float32,
            )
            return (sums, partial_value)

        totals, context_sum = lax.fori_loop(0, block_total, add_block, (totals, context_sum))
        context = context_sum / jnp.transpose(totals)[:, :, None]
        return context.reshape(cell_count, channels).astype(jnp.bfloat16)

    def apply_block(current, micro_pos):
        normed = layer_norm(current, gain_attn).astype(jnp.bfloat16)
        queries = project(normed, query_weight)
        fresh_key = project(normed, key_weight)
        fresh_value = project(normed, value_weight)
        context = attend(queries, fresh_key, fresh_value, micro_pos)
        attn_out = jnp.dot(context, out_weight, preferred_element_type=jnp.float32)
        x_mid = current + attn_out.reshape(row_count, col_count, channels)
        conv_in = jax.nn.silu(layer_norm(x_mid, gain_conv)).astype(jnp.bfloat16)
        edges_now = lax.dynamic_index_in_dim(edge_rows, micro_pos, 0, keepdims=False)
        extended = jnp.concatenate([edges_now[0:1], conv_in, edges_now[3:4]], 0)
        extended = jnp.pad(extended, ((0, 0), (1, 1), (0, 0)))
        conv_sum = jnp.zeros((cell_count, channels), jnp.float32)
        for row_tap in range(3):
            for col_tap in range(3):
                shifted = extended[
                    row_tap : row_tap + row_count, col_tap : col_tap + col_count
                ].reshape(-1, channels)
                conv_sum = conv_sum + jnp.dot(
                    shifted, kernel[row_tap, col_tap], preferred_element_type=jnp.float32
                )
        return x_mid + conv_sum.reshape(row_count, col_count, channels)

    def advance(tick_index, carry):
        incoming, results = carry
        micro = tick_index - segment_index
        active = (micro >= 0) & (micro < micro_count)
        micro_pos = jnp.clip(micro, 0, micro_count - 1)
        first_input = lax.dynamic_index_in_dim(latent, micro_pos, 0, keepdims=False).astype(
            jnp.float32
        )
        block_input = jnp.where(segment_index == 0, first_input, incoming)
        produced = lax.cond(
            active, lambda: apply_block(block_input, micro_pos), lambda: jnp.zeros_like(incoming)
        )
        is_last = active & (segment_index == segment_count - 1)
        results = jnp.where(
            is_last, lax.dynamic_update_index_in_dim(results, produced, micro_pos, 0), results
        )
        incoming = passed_along(produced.astype(jnp.bfloat16), "segment", 1).astype(produced.dtype)
        return (incoming, results)

    start_input = jnp.zeros((row_count, col_count, channels), jnp.float32)
    start_results = jnp.zeros((micro_count, row_count, col_count, channels), jnp.float32)
    final_in, results = lax.fori_loop(
        0, micro_count + segment_count - 1, advance, (start_input, start_results)
    )
    return lax.psum_scatter(
        results.astype(jnp.bfloat16), "segment", scatter_dimension=2, tiled=True
    ).astype(jnp.float32)


def solution(mesh):
    in_specs = (
        P(None, "patch", None, None),
        P("segment", None, "patch", None, None),
        P("segment", None, "patch", None, None),
        P("segment", None),
        P("segment", None, None),
        P("segment", None, None),
        P("segment", None, None),
        P("segment", None, None),
        P("segment", None),
        P("segment", None, None, None, None),
    )
    out_specs = P(None, "patch", "segment", None)
    return jax.shard_map(shards, mesh=mesh, in_specs=in_specs, out_specs=out_specs, check_vma=False)
```

profile of v0, /device:TPU:0, one launch (start us, length us, event | category | flops | bytes accessed | tf_op | source)
XLA Modules:
  0.0 809.1 jit_solution(14509728789227207962)
XLA Ops:
  17.0 3.9 collective-permute-start.1
  24.4 4.3 collective-permute-done.2
  29.6 67.6 %all-gather.3.cloned.1.call-done = bf16[2,64,64,640]{3,2,1,0:T(8,128)(2,1)} async-done(((bf16[2,4,64,640]{3,2,1,0:T(8,128)(2,1)}), bf16[2,64,64,640]{3,2,1,0:T(8,128)(2,1)}) %all-gather.3.cloned.1.call-update) | async-done | bytes 10485776 | tf_op jit(solution)/shard_map/all_gather | solution.py:67
  97.2 14.8 %copy.34 = bf16[2,4096,640]{1,2,0:T(8,128)(2,1)} copy(bf16[2,4096,640]{2,1,0:T(8,128)(2,1)} %bitcast.213) | data formatting | bytes 20971520
  112.1 67.4 %all-gather.5.cloned.1.call-done = bf16[2,64,64,640]{3,2,1,0:T(8,128)(2,1)} async-done(((bf16[2,4,64,640]{3,2,1,0:T(8,128)(2,1)}), bf16[2,64,64,640]{3,2,1,0:T(8,128)(2,1)}) %all-gather.5.cloned.1.call-update) | async-done | bytes 10485776 | tf_op jit(solution)/shard_map/all_gather | solution.py:68
  179.5 14.9 %copy.35 = bf16[2,4096,640]{1,2,0:T(8,128)(2,1)} copy(bf16[2,4096,640]{2,1,0:T(8,128)(2,1)} %bitcast.214) | data formatting | bytes 20971520
  195.4 401.9 %while.41 = (s32[]{:T(128)}, f32[4,64,640]{2,1,0:T(8,128)S(1)}, bf16[2,4,64,640]{3,2,1,0:T(8,128)(2,1)}, s32[]{:T(128)}, pred[]{:T(512)}, /*index=5*/bf16[2,4,64...) while((s32[]{:T(128)}, f32[4,64,640]{2,1,0:T(8,128)S(1)}, ...), condition=%wide.region_13.14_spmd.clone, body=%wide.region_2.13_spmd.clone.sunk | while | flops 3595085824 | bytes 135619984 | solution.py:171
  195.6 58.3 %conditional.3 = (bf16[4,64,640]{2,1,0:T(8,128)(2,1)S(1)}) conditional(s32[]{:T(128)} %convert_element_type.192, () %tuple.104, (pred[]{:T(512)}, bf16[2,4,64,640]{3,2,1,0:T(8,128)(2,1)S(1)}, s32[]{:T(128)}, s32[]{:T(128)}, f32[1,640]{1,0:T(1,128)S(1)}, /*index=5*/bf16[640,640]{1,0:T(8,128)(2,1)}, bf16[640,640]{1,0:T(8,128)(2,1)}, ...), branch_computations={%region_3.3_spmd, %region_4.12_spmd.clone} | conditional | flops 3594758144 | bytes 132342232 | solution.py:159
  204.8 9.7 %dynamic-slice_bitcast_fusion = (bf16[4096,640]{0,1:T(8,128)(2,1)}, bf16[4096,640]{0,1:T(8,128)(2,1)}) fusion(bf16[2,4096,640]{1,2,0:T(8,128)(2,1)} %get-tuple-element.763, s32[]{:T(128)S(6)} %select_n.87, bf16[2,4096,640]{1,2,0:T(8,128)(2,1)} %get-tuple-element.761), kind=kLoop, calls=%fused_computation.22 | loop fusion | bytes 20971524 | tf_op jit(solution)/shard_map/while/body/eval_jaxpr/cond/branch_1_fun/jit(dynamic_index_in_dim)/squeeze | solution.py:79
  214.5 27.1 %while.40 = (s32[]{:T(128)}, f32[10,256]{1,0:T(8,128)S(1)}, f32[256,10,64]{0,2,1:T(8,128)S(1)}, bf16[4096,640]{0,1:T(8,128)(2,1)}, bf16[256,10,64]{0,2,1:T(8,128...) while((s32[]{:T(128)}, f32[10,256]{1,0:T(8,128)S(1)}, ...), condition=%wide.region_10.9_spmd, body=%wide.region_8.8_spmd.sunk | while | flops 686999552 | bytes 30527656 | solution.py:123
  216.6 2.8 bitcast_reduce_fusion.2
  223.3 2.8 bitcast_reduce_fusion.2
  230.1 2.8 bitcast_reduce_fusion.2
  257.1 58.3 %conditional.3 = (bf16[4,64,640]{2,1,0:T(8,128)(2,1)S(1)}) conditional(s32[]{:T(128)} %convert_element_type.192, () %tuple.104, (pred[]{:T(512)}, bf16[2,4,64,640]{3,2,1,0:T(8,128)(2,1)S(1)}, s32[]{:T(128)}, s32[]{:T(128)}, f32[1,640]{1,0:T(1,128)S(1)}, /*index=5*/bf16[640,640]{1,0:T(8,128)(2,1)}, bf16[640,640]{1,0:T(8,128)(2,1)}, ...), branch_computations={%region_3.3_spmd, %region_4.12_spmd.clone} | conditional | flops 3594758144 | bytes 132342232 | solution.py:159
  266.4 9.7 %dynamic-slice_bitcast_fusion = (bf16[4096,640]{0,1:T(8,128)(2,1)}, bf16[4096,640]{0,1:T(8,128)(2,1)}) fusion(bf16[2,4096,640]{1,2,0:T(8,128)(2,1)} %get-tuple-element.763, s32[]{:T(128)S(6)} %select_n.87, bf16[2,4096,640]{1,2,0:T(8,128)(2,1)} %get-tuple-element.761), kind=kLoop, calls=%fused_computation.22 | loop fusion | bytes 20971524 | tf_op jit(solution)/shard_map/while/body/eval_jaxpr/cond/branch_1_fun/jit(dynamic_index_in_dim)/squeeze | solution.py:79
  276.0 27.1 %while.40 = (s32[]{:T(128)}, f32[10,256]{1,0:T(8,128)S(1)}, f32[256,10,64]{0,2,1:T(8,128)S(1)}, bf16[4096,640]{0,1:T(8,128)(2,1)}, bf16[256,10,64]{0,2,1:T(8,128...) while((s32[]{:T(128)}, f32[10,256]{1,0:T(8,128)S(1)}, ...), condition=%wide.region_10.9_spmd, body=%wide.region_8.8_spmd.sunk | while | flops 686999552 | bytes 30527656 | solution.py:123
  319.0 62.4 %collective-permute-start = (bf16[4,64,640]{2,1,0:T(8,128)(2,1)S(1)}, bf16[4,64,640]{2,1,0:T(8,128)(2,1)S(1)}, u32[]{:S(2)}, u32[]{:S(2)}) collective-permute-start(bf16[4,64,640]{2,1,0:T(8,128)(2,1)S(1)} %get-tuple-element.1118), channel_id=1, source_target_pairs={{0,16},{16,32},{32,48},{48,64},{64,80},{80,96},{96,112},{1,17},{17... | collective-permute-start | bytes 983048 | tf_op jit(solution)/shard_map/while/body/eval_jaxpr/ppermute | solution.py:29
  383.4 6.6 collective-permute-start
  391.9 64.8 %collective-permute-start = (bf16[4,64,640]{2,1,0:T(8,128)(2,1)S(1)}, bf16[4,64,640]{2,1,0:T(8,128)(2,1)S(1)}, u32[]{:S(2)}, u32[]{:S(2)}) collective-permute-start(bf16[4,64,640]{2,1,0:T(8,128)(2,1)S(1)} %get-tuple-element.1118), channel_id=1, source_target_pairs={{0,16},{16,32},{32,48},{48,64},{64,80},{80,96},{96,112},{1,17},{17... | collective-permute-start | bytes 983048 | tf_op jit(solution)/shard_map/while/body/eval_jaxpr/ppermute | solution.py:29
  458.7 6.6 collective-permute-start
  467.2 55.3 %collective-permute-start = (bf16[4,64,640]{2,1,0:T(8,128)(2,1)S(1)}, bf16[4,64,640]{2,1,0:T(8,128)(2,1)S(1)}, u32[]{:S(2)}, u32[]{:S(2)}) collective-permute-start(bf16[4,64,640]{2,1,0:T(8,128)(2,1)S(1)} %get-tuple-element.1118), channel_id=1, source_target_pairs={{0,16},{16,32},{32,48},{48,64},{64,80},{80,96},{96,112},{1,17},{17... | collective-permute-start | bytes 983048 | tf_op jit(solution)/shard_map/while/body/eval_jaxpr/ppermute | solution.py:29
  524.5 6.6 collective-permute-start
  533.0 62.4 %collective-permute-start = (bf16[4,64,640]{2,1,0:T(8,128)(2,1)S(1)}, bf16[4,64,640]{2,1,0:T(8,128)(2,1)S(1)}, u32[]{:S(2)}, u32[]{:S(2)}) collective-permute-start(bf16[4,64,640]{2,1,0:T(8,128)(2,1)S(1)} %get-tuple-element.1118), channel_id=1, source_target_pairs={{0,16},{16,32},{32,48},{48,64},{64,80},{80,96},{96,112},{1,17},{17... | collective-permute-start | bytes 983048 | tf_op jit(solution)/shard_map/while/body/eval_jaxpr/ppermute | solution.py:29
  600.2 200.8 %reduce-scatter.4.cloned.1.call-done = bf16[8,5120]{1,0:T(8,128)(2,1)} async-done(((bf16[64,5120]{1,0:T(8,128)(2,1)}), bf16[8,5120]{1,0:T(8,128)(2,1)}) %reduce-scatter.4.cloned.1.call-update) | async-done | bytes 81936
  (202 shorter events, 128.2 us)
Async XLA Ops:
  6.5 10.4 %copy-start.3 = (bf16[1,2,2,64,640]{4,3,2,1,0:T(8,128)(2,1)S(1)}, bf16[1,2,2,64,640]{4,3,2,1,0:T(8,128)(2,1)}, u32[]{:S(2)}) copy-start(bf16[1,2,2,64,640]{4,3,2,1,0:T(8,128)(2,1)} %param.18) | copy-start | bytes 983044
  6.5 90.7 %all-gather.3.cloned.1.call-start = ((), (), s32[]{:S(2)}) async-start(), calls=%async_computation.1 | async-start | bytes 11141120 | tf_op jit(solution)/shard_map/all_gather | solution.py:67
  14.1 165.4 %all-gather.5.cloned.1.call-start = ((), (), s32[]{:S(2)}) async-start(), calls=%async_computation.2 | async-start | bytes 11141120 | tf_op jit(solution)/shard_map/all_gather | solution.py:68
  16.9 784.0 %reduce-scatter.4.cloned.1.call-start = ((), (), s32[]{:S(2)}) async-start(), calls=%async_computation.3 | async-start | bytes 737280
  17.0 7.4 collective-permute-start.1
  20.9 7.7 collective-permute-start.2
  179.5 15.8 %copy-start = (bf16[2,4,64,640]{3,2,1,0:T(8,128)(2,1)S(1)}, bf16[2,4,64,640]{3,2,1,0:T(8,128)(2,1)}, u32[]{:S(2)}) copy-start(bf16[2,4,64,640]{3,2,1,0:T(8,128)(2,1)} %param.16) | copy-start | bytes 1966084
  179.5 15.8 %copy-start.4 = (f32[1,640]{1,0:T(1,128)S(1)}, f32[1,640]{1,0:T(1,128)}, u32[]{:S(2)}) copy-start(f32[1,640]{1,0:T(1,128)} %param.19) | copy-start | bytes 7684
  179.5 15.8 %copy-start.5 = (f32[1,640]{1,0:T(1,128)S(1)}, f32[1,640]{1,0:T(1,128)}, u32[]{:S(2)}) copy-start(f32[1,640]{1,0:T(1,128)} %param.24) | copy-start | bytes 7684
  214.5 27.5 %copy-start.1 = (bf16[640,640]{1,0:T(8,128)(2,1)S(1)}, bf16[640,640]{1,0:T(8,128)(2,1)}, u32[]{:S(2)}) copy-start(bf16[640,640]{1,0:T(8,128)(2,1)} %get-tuple-element.766) | copy-start | bytes 2457604 | tf_op jit(solution)/shard_map/while/body/eval_jaxpr/cond
  244.1 7.3 slice-start
  246.4 5.1 slice-start.1
  253.9 3.1 collective-permute-start
  276.0 27.5 %copy-start.1 = (bf16[640,640]{1,0:T(8,128)(2,1)S(1)}, bf16[640,640]{1,0:T(8,128)(2,1)}, u32[]{:S(2)}) copy-start(bf16[640,640]{1,0:T(8,128)(2,1)} %get-tuple-element.766) | copy-start | bytes 2457604 | tf_op jit(solution)/shard_map/while/body/eval_jaxpr/cond
  305.6 7.3 slice-start
  307.9 5.1 slice-start.1
  315.4 3.5 collective-permute-start
  319.0 64.2 %collective-permute-start = (bf16[4,64,640]{2,1,0:T(8,128)(2,1)S(1)}, bf16[4,64,640]{2,1,0:T(8,128)(2,1)S(1)}, u32[]{:S(2)}, u32[]{:S(2)}) collective-permute-start(bf16[4,64,640]{2,1,0:T(8,128)(2,1)S(1)} %get-tuple-element.1118), channel_id=1, source_target_pairs={{0,16},{16,32},{32,48},{48,64},{64,80},{80,96},{96,112},{1,17},{17... | collective-permute-start | bytes 983048 | tf_op jit(solution)/shard_map/while/body/eval_jaxpr/ppermute | solution.py:29
  383.4 8.4 %collective-permute-start = (bf16[4,64,640]{2,1,0:T(8,128)(2,1)S(1)}, bf16[4,64,640]{2,1,0:T(8,128)(2,1)S(1)}, u32[]{:S(2)}, u32[]{:S(2)}) collective-permute-start(bf16[4,64,640]{2,1,0:T(8,128)(2,1)S(1)} %get-tuple-element.1118), channel_id=1, source_target_pairs={{0,16},{16,32},{32,48},{48,64},{64,80},{80,96},{96,112},{1,17},{17... | collective-permute-start | bytes 983048 | tf_op jit(solution)/shard_map/while/body/eval_jaxpr/ppermute | solution.py:29
  391.9 66.7 %collective-permute-start = (bf16[4,64,640]{2,1,0:T(8,128)(2,1)S(1)}, bf16[4,64,640]{2,1,0:T(8,128)(2,1)S(1)}, u32[]{:S(2)}, u32[]{:S(2)}) collective-permute-start(bf16[4,64,640]{2,1,0:T(8,128)(2,1)S(1)} %get-tuple-element.1118), channel_id=1, source_target_pairs={{0,16},{16,32},{32,48},{48,64},{64,80},{80,96},{96,112},{1,17},{17... | collective-permute-start | bytes 983048 | tf_op jit(solution)/shard_map/while/body/eval_jaxpr/ppermute | solution.py:29
  458.7 8.4 %collective-permute-start = (bf16[4,64,640]{2,1,0:T(8,128)(2,1)S(1)}, bf16[4,64,640]{2,1,0:T(8,128)(2,1)S(1)}, u32[]{:S(2)}, u32[]{:S(2)}) collective-permute-start(bf16[4,64,640]{2,1,0:T(8,128)(2,1)S(1)} %get-tuple-element.1118), channel_id=1, source_target_pairs={{0,16},{16,32},{32,48},{48,64},{64,80},{80,96},{96,112},{1,17},{17... | collective-permute-start | bytes 983048 | tf_op jit(solution)/shard_map/while/body/eval_jaxpr/ppermute | solution.py:29
  467.2 57.1 %collective-permute-start = (bf16[4,64,640]{2,1,0:T(8,128)(2,1)S(1)}, bf16[4,64,640]{2,1,0:T(8,128)(2,1)S(1)}, u32[]{:S(2)}, u32[]{:S(2)}) collective-permute-start(bf16[4,64,640]{2,1,0:T(8,128)(2,1)S(1)} %get-tuple-element.1118), channel_id=1, source_target_pairs={{0,16},{16,32},{32,48},{48,64},{64,80},{80,96},{96,112},{1,17},{17... | collective-permute-start | bytes 983048 | tf_op jit(solution)/shard_map/while/body/eval_jaxpr/ppermute | solution.py:29
  524.5 8.4 %collective-permute-start = (bf16[4,64,640]{2,1,0:T(8,128)(2,1)S(1)}, bf16[4,64,640]{2,1,0:T(8,128)(2,1)S(1)}, u32[]{:S(2)}, u32[]{:S(2)}) collective-permute-start(bf16[4,64,640]{2,1,0:T(8,128)(2,1)S(1)} %get-tuple-element.1118), channel_id=1, source_target_pairs={{0,16},{16,32},{32,48},{48,64},{64,80},{80,96},{96,112},{1,17},{17... | collective-permute-start | bytes 983048 | tf_op jit(solution)/shard_map/while/body/eval_jaxpr/ppermute | solution.py:29
  533.0 64.2 %collective-permute-start = (bf16[4,64,640]{2,1,0:T(8,128)(2,1)S(1)}, bf16[4,64,640]{2,1,0:T(8,128)(2,1)S(1)}, u32[]{:S(2)}, u32[]{:S(2)}) collective-permute-start(bf16[4,64,640]{2,1,0:T(8,128)(2,1)S(1)} %get-tuple-element.1118), channel_id=1, source_target_pairs={{0,16},{16,32},{32,48},{48,64},{64,80},{80,96},{96,112},{1,17},{17... | collective-permute-start | bytes 983048 | tf_op jit(solution)/shard_map/while/body/eval_jaxpr/ppermute | solution.py:29
  (2 other events, 4.8 us)
Sparse Core Ops, SparseCore 0:
  14.2 82.9 all-gather.2
  99.4 80.0 all-gather.4
  600.3 200.6 reduce-scatter.3
where the time goes:
time: 811 us; the launch traced here: 809 us
  waiting for transfers between devices  342 us (42%)
  starting transfers between devices  273 us (34%)
  matrix products  78.8 us (10%)
  local copies, waits for them, and re-layouts  74 us (9%)
  other arithmetic  26 us (3%)
  between operations  13.2 us (2%)
    ppermute x9, starting transfers between devices, passed_along(): return lax.ppermute(value, axis, pairs)  268 us
    unnamed x4, waiting for transfers between devices  201 us
    all_gather x1, waiting for transfers between devices, shards(): lax.all_gather(near_keys, 'patch', axis=1, tiled=True)  67.6 us
    all_gather x1, waiting for transfers between devices, shards(): lax.all_gather(near_values, 'patch', axis=1, tiled=True)  67.4 us
    unnamed x13, local copies, waits for them, and re-layouts  33.6 us
    dot_general x8, matrix products, add_block(): jnp.einsum('qhd,khd->hqk', query_heads, key_part, preferred_element_type=...  22.5 us
    squeeze x2, local copies, waits for them, and re-layouts, attend(): lax.dynamic_index_in_dim(far_values, micro_pos, 0, keepdims=False)  19.3 us
    dot_general x18, matrix products, apply_block(): jnp.dot(shifted, kernel[row_tap, col_tap], preferred_element_type=jnp.flo...  18.2 us
  transfers between devices with their start and end apart: 14, of which 5 were waited for; matrix products, arithmetic and copies ran while one was open for 4% of the time, Pallas kernels for 0%

commit v1 on v0

--- a/solution.py
+++ b/solution.py
@@ -64,7 +64,9 @@
     near_keys = project(stale_normed, key_weight)
     near_values = project(stale_normed, value_weight)
     far_keys, far_values = (
-        lax.all_gather(near_keys, "patch", axis=1, tiled=True),
+        jnp.concatenate(
+            lax.all_to_all(jnp.stack([near_keys] * lax.axis_size("patch")), "patch", 0, 0), axis=1
+        ),
         lax.all_gather(near_values, "patch", axis=1, tiled=True),
     )
     far_keys = far_keys.reshape(micro_count, -1, channels)

time: 811 us -> 901 us (1.11)
  waiting for transfers between devices: 342 us -> 410 us
  local copies, waits for them, and re-layouts: 74 us -> 88.7 us
    ppermute x1, waiting for transfers between devices: 2.11 us -> 113 us  [padded(): lax.ppermute(tail, axis, [(i, (i + 1) % count) for i in range(ends)])]
    all_to_all x0 -> x1, waiting for transfers between devices: none -> 90.4 us  [shards(): lax.all_to_all(jnp.stack([near_keys] * lax.axis_size('patch')), 'patch',...]
    all_gather x1 -> x0, waiting for transfers between devices: 67.6 us -> none  [shards(): lax.all_gather(near_keys, 'patch', axis=1, tiled=True)]
    all_gather x1, waiting for transfers between devices: 67.4 us -> 0.01 us  [shards(): lax.all_gather(near_values, 'patch', axis=1, tiled=True)]
    all_to_all x0 -> x1, local copies, waits for them, and re-layouts: none -> 9.43 us  [shards(): lax.all_to_all(jnp.stack([near_keys] * lax.axis_size('patch')), 'patch',...]
    unnamed x4 -> x3, waiting for transfers between devices: 201 us -> 203 us
  transfers between devices with their start and end apart: 14 -> 14, of which waited for: 5 -> 4; matrix products, arithmetic and copies ran while one was open for 4% -> 5% of each run, Pallas kernels for 0% -> 0%
where the time goes in v1:
time: 901 us; the launch traced here: 899 us
  waiting for transfers between devices  410 us (46%)
  starting transfers between devices  281 us (31%)
  local copies, waits for them, and re-layouts  88.7 us (10%)
  matrix products  78 us (9%)
  other arithmetic  26 us (3%)
  between operations  13.5 us (1%)
    ppermute x9, starting transfers between devices, passed_along(): return lax.ppermute(value, axis, pairs)  268 us
    unnamed x3, waiting for transfers between devices  203 us
    ppermute x1, waiting for transfers between devices, padded(): lax.ppermute(tail, axis, [(i, (i + 1) % count) for i in range(ends)])  113 us
    all_to_all x1, waiting for transfers between devices, shards(): lax.all_to_all(jnp.stack([near_keys] * lax.axis_size('patch')), 'patch',...  90.4 us
    unnamed x13, local copies, waits for them, and re-layouts  33.5 us
    dot_general x8, matrix products, add_block(): jnp.einsum('qhd,khd->hqk', query_heads, key_part, preferred_element_type=...  22.5 us
    squeeze x2, local copies, waits for them, and re-layouts, attend(): lax.dynamic_index_in_dim(far_values, micro_pos, 0, keepdims=False)  19.4 us
    dot_general x18, matrix products, apply_block(): jnp.dot(shifted, kernel[row_tap, col_tap], preferred_element_type=jnp.flo...  18.2 us
  transfers between devices with their start and end apart: 14, of which 4 were waited for; matrix products, arithmetic and copies ran while one was open for 5% of the time, Pallas kernels for 0%

profile of v1, /device:TPU:0, one launch (start us, length us, event | category | flops | bytes accessed | tf_op | source)
XLA Modules:
  0.0 899.1 jit_solution(3511886098156032012)
XLA Ops:
  16.0 5.4 stack.3
  21.4 8.3 all-to-all-start
  29.8 3.8 collective-permute-start.1
  34.9 113.5 %collective-permute-done.1 = bf16[2,1,64,640]{3,2,1,0:T(8,128)(2,1)S(1)} collective-permute-done((bf16[2,1,64,640]{3,2,1,0:T(8,128)(2,1)S(1)}, bf16[2,1,64,640]{3,2,1,0:T(8,128)(2,1)S(1)}, u32[]{:S(2)}, u32[]{:S(2)}) %collective-permute-start.1) | collective-permute-done | bytes 163872 | tf_op jit(solution)/shard_map/ppermute | solution.py:17
  148.4 3.2 collective-permute-done.2
  152.5 90.4 %all-to-all-done = bf16[16,2,4,64,640]{4,3,2,1,0:T(8,128)(2,1)} async-done(((bf16[16,2,4,64,640]{4,3,2,1,0:T(8,128)(2,1)}), bf16[16,2,4,64,640]{4,3,2,1,0:T(8,128)(2,1)}, u32[]{:S(2)}, u32[]{:S(2)}) %all-to-all-start) | async-done | bytes 10485792 | tf_op jit(solution)/shard_map/all_to_all | solution.py:68
  242.8 9.4 %copy.34 = bf16[16,2,4,64,640]{4,3,2,0,1:T(8,128)(2,1)} copy(bf16[16,2,4,64,640]{4,3,2,1,0:T(8,128)(2,1)} %all-to-all-done) | data formatting | bytes 20971520 | tf_op jit(solution)/shard_map/all_to_all | solution.py:68
  252.3 14.7 %copy.35 = bf16[2,4096,640]{1,2,0:T(8,128)(2,1)} copy(bf16[2,4096,640]{2,1,0:T(8,128)(2,1)} %bitcast.201) | data formatting | bytes 20971520
  267.0 14.9 %copy.36 = bf16[2,4096,640]{1,2,0:T(8,128)(2,1)} copy(bf16[2,4096,640]{2,1,0:T(8,128)(2,1)} %bitcast.216) | data formatting | bytes 20971520
  282.9 401.8 %while.41 = (s32[]{:T(128)}, f32[4,64,640]{2,1,0:T(8,128)S(1)}, bf16[2,4,64,640]{3,2,1,0:T(8,128)(2,1)}, s32[]{:T(128)}, pred[]{:T(512)}, /*index=5*/bf16[2,4,64...) while((s32[]{:T(128)}, f32[4,64,640]{2,1,0:T(8,128)S(1)}, ...), condition=%wide.region_13.14_spmd.clone, body=%wide.region_2.13_spmd.clone.sunk | while | flops 3595085824 | bytes 135619984 | solution.py:173
  283.1 58.3 %conditional.3 = (bf16[4,64,640]{2,1,0:T(8,128)(2,1)S(1)}) conditional(s32[]{:T(128)} %convert_element_type.192, () %tuple.104, (pred[]{:T(512)}, bf16[2,4,64,640]{3,2,1,0:T(8,128)(2,1)S(1)}, s32[]{:T(128)}, s32[]{:T(128)}, f32[1,640]{1,0:T(1,128)S(1)}, /*index=5*/bf16[640,640]{1,0:T(8,128)(2,1)}, bf16[640,640]{1,0:T(8,128)(2,1)}, ...), branch_computations={%region_3.3_spmd, %region_4.12_spmd.clone} | conditional | flops 3594758144 | bytes 132342232 | solution.py:161
  292.3 9.7 %dynamic-slice_bitcast_fusion = (bf16[4096,640]{0,1:T(8,128)(2,1)}, bf16[4096,640]{0,1:T(8,128)(2,1)}) fusion(bf16[2,4096,640]{1,2,0:T(8,128)(2,1)} %get-tuple-element.763, s32[]{:T(128)S(6)} %select_n.87, bf16[2,4096,640]{1,2,0:T(8,128)(2,1)} %get-tuple-element.761), kind=kLoop, calls=%fused_computation.22 | loop fusion | bytes 20971524 | tf_op jit(solution)/shard_map/while/body/eval_jaxpr/cond/branch_1_fun/jit(dynamic_index_in_dim)/squeeze | solution.py:81
  302.0 27.1 %while.40 = (s32[]{:T(128)}, f32[10,256]{1,0:T(8,128)S(1)}, f32[256,10,64]{0,2,1:T(8,128)S(1)}, bf16[4096,640]{0,1:T(8,128)(2,1)}, bf16[256,10,64]{0,2,1:T(8,128...) while((s32[]{:T(128)}, f32[10,256]{1,0:T(8,128)S(1)}, ...), condition=%wide.region_10.9_spmd, body=%wide.region_8.8_spmd.sunk | while | flops 686999552 | bytes 30527656 | solution.py:125
  344.6 58.3 %conditional.3 = (bf16[4,64,640]{2,1,0:T(8,128)(2,1)S(1)}) conditional(s32[]{:T(128)} %convert_element_type.192, () %tuple.104, (pred[]{:T(512)}, bf16[2,4,64,640]{3,2,1,0:T(8,128)(2,1)S(1)}, s32[]{:T(128)}, s32[]{:T(128)}, f32[1,640]{1,0:T(1,128)S(1)}, /*index=5*/bf16[640,640]{1,0:T(8,128)(2,1)}, bf16[640,640]{1,0:T(8,128)(2,1)}, ...), branch_computations={%region_3.3_spmd, %region_4.12_spmd.clone} | conditional | flops 3594758144 | bytes 132342232 | solution.py:161
  353.8 9.7 %dynamic-slice_bitcast_fusion = (bf16[4096,640]{0,1:T(8,128)(2,1)}, bf16[4096,640]{0,1:T(8,128)(2,1)}) fusion(bf16[2,4096,640]{1,2,0:T(8,128)(2,1)} %get-tuple-element.763, s32[]{:T(128)S(6)} %select_n.87, bf16[2,4096,640]{1,2,0:T(8,128)(2,1)} %get-tuple-element.761), kind=kLoop, calls=%fused_computation.22 | loop fusion | bytes 20971524 | tf_op jit(solution)/shard_map/while/body/eval_jaxpr/cond/branch_1_fun/jit(dynamic_index_in_dim)/squeeze | solution.py:81
  363.5 27.1 %while.40 = (s32[]{:T(128)}, f32[10,256]{1,0:T(8,128)S(1)}, f32[256,10,64]{0,2,1:T(8,128)S(1)}, bf16[4096,640]{0,1:T(8,128)(2,1)}, bf16[256,10,64]{0,2,1:T(8,128...) while((s32[]{:T(128)}, f32[10,256]{1,0:T(8,128)S(1)}, ...), condition=%wide.region_10.9_spmd, body=%wide.region_8.8_spmd.sunk | while | flops 686999552 | bytes 30527656 | solution.py:125
  406.5 62.4 %collective-permute-start = (bf16[4,64,640]{2,1,0:T(8,128)(2,1)S(1)}, bf16[4,64,640]{2,1,0:T(8,128)(2,1)S(1)}, u32[]{:S(2)}, u32[]{:S(2)}) collective-permute-start(bf16[4,64,640]{2,1,0:T(8,128)(2,1)S(1)} %get-tuple-element.1118), channel_id=1, source_target_pairs={{0,16},{16,32},{32,48},{48,64},{64,80},{80,96},{96,112},{1,17},{17... | collective-permute-start | bytes 983048 | tf_op jit(solution)/shard_map/while/body/eval_jaxpr/ppermute | solution.py:29
  470.8 6.6 collective-permute-start
  479.4 64.8 %collective-permute-start = (bf16[4,64,640]{2,1,0:T(8,128)(2,1)S(1)}, bf16[4,64,640]{2,1,0:T(8,128)(2,1)S(1)}, u32[]{:S(2)}, u32[]{:S(2)}) collective-permute-start(bf16[4,64,640]{2,1,0:T(8,128)(2,1)S(1)} %get-tuple-element.1118), channel_id=1, source_target_pairs={{0,16},{16,32},{32,48},{48,64},{64,80},{80,96},{96,112},{1,17},{17... | collective-permute-start | bytes 983048 | tf_op jit(solution)/shard_map/while/body/eval_jaxpr/ppermute | solution.py:29
  546.1 6.6 collective-permute-start
  554.7 55.3 %collective-permute-start = (bf16[4,64,640]{2,1,0:T(8,128)(2,1)S(1)}, bf16[4,64,640]{2,1,0:T(8,128)(2,1)S(1)}, u32[]{:S(2)}, u32[]{:S(2)}) collective-permute-start(bf16[4,64,640]{2,1,0:T(8,128)(2,1)S(1)} %get-tuple-element.1118), channel_id=1, source_target_pairs={{0,16},{16,32},{32,48},{48,64},{64,80},{80,96},{96,112},{1,17},{17... | collective-permute-start | bytes 983048 | tf_op jit(solution)/shard_map/while/body/eval_jaxpr/ppermute | solution.py:29
  611.9 6.6 collective-permute-start
  620.5 62.4 %collective-permute-start = (bf16[4,64,640]{2,1,0:T(8,128)(2,1)S(1)}, bf16[4,64,640]{2,1,0:T(8,128)(2,1)S(1)}, u32[]{:S(2)}, u32[]{:S(2)}) collective-permute-start(bf16[4,64,640]{2,1,0:T(8,128)(2,1)S(1)} %get-tuple-element.1118), channel_id=1, source_target_pairs={{0,16},{16,32},{32,48},{48,64},{64,80},{80,96},{96,112},{1,17},{17... | collective-permute-start | bytes 983048 | tf_op jit(solution)/shard_map/while/body/eval_jaxpr/ppermute | solution.py:29
  687.6 203.0 %reduce-scatter.4.cloned.1.call-done = bf16[8,5120]{1,0:T(8,128)(2,1)} async-done(((bf16[64,5120]{1,0:T(8,128)(2,1)}), bf16[8,5120]{1,0:T(8,128)(2,1)}) %reduce-scatter.4.cloned.1.call-update) | async-done | bytes 81936
  (203 shorter events, 133.6 us)
Async XLA Ops:
  6.5 260.5 %all-gather.2.cloned.1.call-start = ((), (), s32[]{:S(2)}) async-start(), calls=%async_computation.2 | async-start | bytes 11141120 | tf_op jit(solution)/shard_map/all_gather | solution.py:70
  21.4 8.4 copy-start.3
  21.4 221.5 %all-to-all-start = ((bf16[16,2,4,64,640]{4,3,2,1,0:T(8,128)(2,1)}), bf16[16,2,4,64,640]{4,3,2,1,0:T(8,128)(2,1)}, u32[]{:S(2)}, u32[]{:S(2)}) async-start(bf16[16,2,4,64,640]{4,3,2,1,0:T(8,128)(2,1)} %stack.3), calls=%async_computation | async-start | bytes 20971520 | tf_op jit(solution)/shard_map/all_to_all | solution.py:68
  29.7 860.9 %reduce-scatter.4.cloned.1.call-start = ((), (), s32[]{:S(2)}) async-start(), calls=%async_computation.3 | async-start | bytes 737280
  29.8 118.6 %collective-permute-start.1 = (bf16[2,1,64,640]{3,2,1,0:T(8,128)(2,1)S(1)}, bf16[2,1,64,640]{3,2,1,0:T(8,128)(2,1)S(1)}, u32[]{:S(2)}, u32[]{:S(2)}) collective-permute-start(bf16[2,1,64,640]{3,2,1,0:T(8,128)(2,1)S(1)} %get-tuple-element.860), channel_id=1, source_target_pairs={{0,1},{1,2},{2,3},{3,4},{4,5},{5,6},{6,7},{7,8},{8,9},{9,10},{10,1... | collective-permute-start | bytes 491528 | tf_op jit(solution)/shard_map/ppermute | solution.py:17
  33.6 118.0 %collective-permute-start.2 = (bf16[2,1,64,640]{3,2,1,0:T(8,128)(2,1)S(1)}, bf16[2,1,64,640]{3,2,1,0:T(8,128)(2,1)S(1)}, u32[]{:S(2)}, u32[]{:S(2)}) collective-permute-start(bf16[2,1,64,640]{3,2,1,0:T(8,128)(2,1)S(1)} %get-tuple-element.861), channel_id=1, source_target_pairs={{1,0},{2,1},{3,2},{4,3},{5,4},{6,5},{7,6},{8,7},{9,8},{10,9},{11,1... | collective-permute-start | bytes 491528 | tf_op jit(solution)/shard_map/ppermute | solution.py:19
  267.0 15.8 %copy-start = (bf16[2,4,64,640]{3,2,1,0:T(8,128)(2,1)S(1)}, bf16[2,4,64,640]{3,2,1,0:T(8,128)(2,1)}, u32[]{:S(2)}) copy-start(bf16[2,4,64,640]{3,2,1,0:T(8,128)(2,1)} %param.16) | copy-start | bytes 1966084
  267.0 15.8 %copy-start.4 = (f32[1,640]{1,0:T(1,128)S(1)}, f32[1,640]{1,0:T(1,128)}, u32[]{:S(2)}) copy-start(f32[1,640]{1,0:T(1,128)} %param.19) | copy-start | bytes 7684
  267.0 15.8 %copy-start.5 = (f32[1,640]{1,0:T(1,128)S(1)}, f32[1,640]{1,0:T(1,128)}, u32[]{:S(2)}) copy-start(f32[1,640]{1,0:T(1,128)} %param.24) | copy-start | bytes 7684
  283.1 6.3 copy-start.2
  302.0 27.5 %copy-start.1 = (bf16[640,640]{1,0:T(8,128)(2,1)S(1)}, bf16[640,640]{1,0:T(8,128)(2,1)}, u32[]{:S(2)}) copy-start(bf16[640,640]{1,0:T(8,128)(2,1)} %get-tuple-element.766) | copy-start | bytes 2457604 | tf_op jit(solution)/shard_map/while/body/eval_jaxpr/cond
  331.6 7.3 slice-start
  341.4 3.1 collective-permute-start
  344.6 6.3 copy-start.2
  363.5 27.5 %copy-start.1 = (bf16[640,640]{1,0:T(8,128)(2,1)S(1)}, bf16[640,640]{1,0:T(8,128)(2,1)}, u32[]{:S(2)}) copy-start(bf16[640,640]{1,0:T(8,128)(2,1)} %get-tuple-element.766) | copy-start | bytes 2457604 | tf_op jit(solution)/shard_map/while/body/eval_jaxpr/cond
  393.1 7.3 slice-start
  402.9 3.5 collective-permute-start
  406.5 64.2 %collective-permute-start = (bf16[4,64,640]{2,1,0:T(8,128)(2,1)S(1)}, bf16[4,64,640]{2,1,0:T(8,128)(2,1)S(1)}, u32[]{:S(2)}, u32[]{:S(2)}) collective-permute-start(bf16[4,64,640]{2,1,0:T(8,128)(2,1)S(1)} %get-tuple-element.1118), channel_id=1, source_target_pairs={{0,16},{16,32},{32,48},{48,64},{64,80},{80,96},{96,112},{1,17},{17... | collective-permute-start | bytes 983048 | tf_op jit(solution)/shard_map/while/body/eval_jaxpr/ppermute | solution.py:29
  470.8 8.4 collective-permute-start
  479.4 66.6 %collective-permute-start = (bf16[4,64,640]{2,1,0:T(8,128)(2,1)S(1)}, bf16[4,64,640]{2,1,0:T(8,128)(2,1)S(1)}, u32[]{:S(2)}, u32[]{:S(2)}) collective-permute-start(bf16[4,64,640]{2,1,0:T(8,128)(2,1)S(1)} %get-tuple-element.1118), channel_id=1, source_target_pairs={{0,16},{16,32},{32,48},{48,64},{64,80},{80,96},{96,112},{1,17},{17... | collective-permute-start | bytes 983048 | tf_op jit(solution)/shard_map/while/body/eval_jaxpr/ppermute | solution.py:29
  546.1 8.4 collective-permute-start
  554.7 57.1 %collective-permute-start = (bf16[4,64,640]{2,1,0:T(8,128)(2,1)S(1)}, bf16[4,64,640]{2,1,0:T(8,128)(2,1)S(1)}, u32[]{:S(2)}, u32[]{:S(2)}) collective-permute-start(bf16[4,64,640]{2,1,0:T(8,128)(2,1)S(1)} %get-tuple-element.1118), channel_id=1, source_target_pairs={{0,16},{16,32},{32,48},{48,64},{64,80},{80,96},{96,112},{1,17},{17... | collective-permute-start | bytes 983048 | tf_op jit(solution)/shard_map/while/body/eval_jaxpr/ppermute | solution.py:29
  611.9 8.4 collective-permute-start
  620.5 64.2 %collective-permute-start = (bf16[4,64,640]{2,1,0:T(8,128)(2,1)S(1)}, bf16[4,64,640]{2,1,0:T(8,128)(2,1)S(1)}, u32[]{:S(2)}, u32[]{:S(2)}) collective-permute-start(bf16[4,64,640]{2,1,0:T(8,128)(2,1)S(1)} %get-tuple-element.1118), channel_id=1, source_target_pairs={{0,16},{16,32},{32,48},{48,64},{64,80},{80,96},{96,112},{1,17},{17... | collective-permute-start | bytes 983048 | tf_op jit(solution)/shard_map/while/body/eval_jaxpr/ppermute | solution.py:29
  (2 other events, 10.2 us)
Sparse Core Ops, SparseCore 0:
  14.2 230.7 all-gather.1
  687.8 202.8 reduce-scatter.3
